TPU v7x, 32 devices: a whole 2x2x4 slice. The times are simulated.
32 devices in a mesh: expert: 8 (over z, y), replica: 4 (over x, core).
Axes of the slice: x: 2, y: 2, z: 4, core: 2. Of those that a mesh axis runs over, the one named last changes fastest.
Arguments:
- tokens: bfloat16 [4096, 2048], P(('expert', 'replica')), may hold values from -6 to 6
- expert_ids: int32 [4096, 8], P(('expert', 'replica')), may hold values from 0 to 31, as said below
- gates: float32 [4096, 8], P(('expert', 'replica')), may hold values from 0.02 to 0.25
- cotangent: bfloat16 [4096, 2048], P(('expert', 'replica')), may hold values from -6 to 6
- expert_weights: bfloat16 [32, 2048, 1152], P(('expert', 'replica')), may hold values from -0.125 to 0.125
- moment_first: bfloat16 [32, 2048, 1152], P(('expert', 'replica')), may hold values from -0.00021362305 to 0.00021362305
- moment_second: bfloat16 [32, 2048, 1152], P(('expert', 'replica')), may hold values from 1.3242243e-09 to 1.3213139e-08
- hot_slot: int32 [8], P('expert'), may hold values from 0 to 3
Outputs:
- mixed: bfloat16 [4096, 2048], P(('expert', 'replica'))
- input_grad: bfloat16 [4096, 2048], P(('expert', 'replica'))
- gate_grad: float32 [4096, 8], P(('expert', 'replica'))
- new_weights: bfloat16 [32, 2048, 1152], P(('expert', 'replica'))
- hot_copy: bfloat16 [32, 2048, 1152], P(('expert', 'replica'))
Inputs may be any that keep to these rules, and one draw needn't show every extreme that they name: `expert_ids`: each token names 8 different experts. Experts form 8 groups of 4 consecutive numbers. Of the choices of the 128 tokens of one device (aligned blocks of rows), exactly 128 name experts of each group; in group a the expert a * 4 + hot_slot[a] is named exactly 64 times, every other expert at most 32 times, and one of them exactly 32 times.
All inputs are finite; a program needn't handle non-finite values.
Results may differ from a plain program's by a relative error of at most 0.011.
Values may be sent and summed in bfloat16 or wider, within the bound.
No kernel may reach another device: no remote copies, remote signals or barrier semaphores. Data moves between devices by JAX's collectives and lax.ppermute only.
A program may use at most 256 MiB of HBM per device.

v0:
```python
import jax
import jax.numpy as jnp
from jax import lax
from jax.sharding import PartitionSpec as P

beta_first = 0.9
beta_second = 0.95
adam_eps = 1e-08
rate = 0.05
clip_norm = 1.0
bias_first = 1.0 - 0.9**10
bias_second = 1.0 - 0.95**10


def broadcast(value, axis, source):
    kept = jnp.where(lax.axis_index(axis) == source, value, 0).astype(value.dtype)
    return lax.psum(kept, axis)


def expert_forward(row_block, weights, hidden_width):
    gate_up = jnp.dot(row_block, weights[:, : 2 * hidden_width], preferred_element_type=jnp.float32)
    gate_in = gate_up[:, :hidden_width]
    up_part = gate_up[:, hidden_width:]
    hidden = (gate_in * jax.nn.sigmoid(gate_in) * up_part).astype(jnp.bfloat16)
    outputs = lax.dot_general(
        hidden,
        weights[:, 2 * hidden_width :],
        (((1,), (1,)), ((), ())),
        preferred_element_type=jnp.float32,
    ).astype(jnp.bfloat16)
    return (outputs, gate_up, hidden)


def expert_backward(cot_block, gate_up, weights, hidden_width):
    gate_in = gate_up[:, :hidden_width]
    up_part = gate_up[:, hidden_width:]
    sigmoid_gate = jax.nn.sigmoid(gate_in)
    hidden_grad = jnp.dot(
        cot_block, weights[:, 2 * hidden_width :], preferred_element_type=jnp.float32
    )
    grad_gate = hidden_grad * up_part * sigmoid_gate * (1.0 + gate_in * (1.0 - sigmoid_gate))
    grad_up = hidden_grad * gate_in * sigmoid_gate
    input_both = jnp.concatenate([grad_gate, grad_up], axis=1).astype(jnp.bfloat16)
    slot_grads = lax.dot_general(
        input_both,
        weights[:, : 2 * hidden_width],
        (((1,), (1,)), ((), ())),
        preferred_element_type=jnp.float32,
    ).astype(jnp.bfloat16)
    return (slot_grads, input_both)


def partial_sums(row_block, cot_block, input_both, hidden, leading):
    in_part = jnp.einsum(
        "arcd,arcg->rdg",
        row_block.reshape(leading + (-1,)),
        input_both.reshape(leading + (-1,)),
        preferred_element_type=jnp.float32,
    )
    down_part = jnp.einsum(
        "arcd,arcf->rdf",
        cot_block.reshape(leading + (-1,)),
        hidden.reshape(leading + (-1,)),
        preferred_element_type=jnp.float32,
    )
    partial_value = lax.optimization_barrier(
        jnp.concatenate([in_part, down_part], axis=2).astype(jnp.bfloat16)
    )
    return jnp.sum(partial_value.astype(jnp.float32), axis=0)


def place_slots(target, bins, room, allowed):
    one_hot = (target[:, None] == jnp.arange(bins, dtype=jnp.int32)[None, :]).astype(
        jnp.int32
    ) * allowed[:, None].astype(jnp.int32)
    ahead = jnp.cumsum(one_hot, axis=0) - one_hot
    return target * room + jnp.sum(ahead * one_hot, axis=1)


def to_experts(row_block):
    return lax.all_to_all(row_block, ("expert", "replica"), split_axis=0, concat_axis=0, tiled=True)


def from_experts(row_block):
    return lax.all_to_all(row_block, ("expert", "replica"), split_axis=0, concat_axis=0, tiled=True)


def shards(
    tokens, expert_ids, gates, cotangent, expert_weights, moment_first, moment_second, hot_slot
):
    groups = lax.axis_size("expert")
    owners = lax.axis_size("replica")
    experts = groups * owners
    token_count, chosen = expert_ids.shape
    slot_total = token_count * chosen
    hidden_width = expert_weights.shape[2] // 3
    capacity = 2 * slot_total // experts
    weights = expert_weights[0]
    routed = expert_ids.reshape(-1)
    slot_numbers = jnp.arange(slot_total, dtype=jnp.int32)
    zero_half = jnp.zeros((), jnp.bfloat16)
    all_true = jnp.ones((slot_total,), jnp.bool_)
    hot_member = hot_slot[0]
    slot_place = place_slots(routed, experts, capacity, all_true)
    slot_source = jnp.zeros((experts * capacity,), jnp.int32).at[slot_place].set(slot_numbers)
    slot_filled = jnp.zeros((experts * capacity,), jnp.bool_).at[slot_place].set(True)
    arrived = to_experts(jnp.where(slot_filled[:, None], tokens[slot_source // chosen], zero_half))
    outputs, gate_up, hidden = expert_forward(arrived, weights, hidden_width)
    slot_out = from_experts(outputs)[slot_place]
    slot_wide = slot_out.astype(jnp.float32).reshape(token_count, chosen, -1)
    mixed = jnp.einsum("tk,tkd->td", gates, slot_wide).astype(jnp.bfloat16)
    gate_grad = jnp.einsum("td,tkd->tk", cotangent.astype(jnp.float32), slot_wide)
    slot_cot = (
        (gates[:, :, None] * cotangent[:, None, :].astype(jnp.float32))
        .astype(jnp.bfloat16)
        .reshape(slot_total, -1)
    )
    cot_arrived = to_experts(jnp.where(slot_filled[:, None], slot_cot[slot_source], zero_half))
    slot_grads, input_both = expert_backward(cot_arrived, gate_up, weights, hidden_width)
    gradient = partial_sums(arrived, cot_arrived, input_both, hidden, (groups, owners, capacity))
    slot_dx = from_experts(slot_grads)[slot_place]
    input_grad = jnp.sum(
        slot_dx.astype(jnp.float32).reshape(token_count, chosen, -1), axis=1
    ).astype(jnp.bfloat16)
    clip_bound = clip_norm * experts ** (-0.5)
    scale = jnp.minimum(1.0, clip_bound / (jnp.sqrt(jnp.sum(gradient * gradient)) + 1e-06))
    scaled = scale * gradient
    first = beta_first * moment_first[0].astype(jnp.float32) + (1.0 - beta_first) * scaled
    second = (
        beta_second * moment_second[0].astype(jnp.float32) + (1.0 - beta_second) * scaled * scaled
    )
    update = first / bias_first / (jnp.sqrt(second / bias_second) + adam_eps)
    new_weights = (weights.astype(jnp.float32) - rate * update).astype(jnp.bfloat16)
    hot_copy = broadcast(new_weights, "replica", hot_member)
    return (mixed, input_grad, gate_grad, new_weights[None], hot_copy[None])


def solution(mesh):
    return jax.shard_map(
        shards,
        mesh=mesh,
        in_specs=(
            P(("expert", "replica"), None),
            P(("expert", "replica"), None),
            P(("expert", "replica"), None),
            P(("expert", "replica"), None),
            P(("expert", "replica"), None, None),
            P(("expert", "replica"), None, None),
            P(("expert", "replica"), None, None),
            P("expert"),
        ),
        out_specs=(
            P(("expert", "replica"), None),
            P(("expert", "replica"), None),
            P(("expert", "replica"), None),
            P(("expert", "replica"), None, None),
            P(("expert", "replica"), None, None),
        ),
        check_vma=False,
    )
```

profile of v0, /device:TPU:0, one launch (start us, length us, event | category | flops | bytes accessed | tf_op | source)
XLA Modules:
  0.0 949.9 jit_solution(18028048421142596829)
XLA Ops:
  8.9 9.0 reduce-window.6
  31.9 19.1 %gather_fusion.2 = bf16[2048,2048]{1,0:T(8,128)(2,1)} fusion(bf16[1024,2048]{1,0:T(8,128)(2,1)} %fusion.19, s32[2048]{0:T(1024)S(1)} %get-tuple-element.13), kind=kCustom, calls=%fused_computation.2 | custom fusion | bytes 16785408 | tf_op jit(solution)/shard_map/gather | solution.py:118
  51.0 11.0 %gather_fusion = bf16[2048,2048]{1,0:T(8,128)(2,1)} fusion(bf16[128,2048]{1,0:T(8,128)(2,1)S(1)} %copy-done, s32[2048]{0:T(1024)S(1)} %get-tuple-element.14), kind=kCustom, calls=%fused_computation | custom fusion | bytes 16785408 | tf_op jit(solution)/shard_map/gather | solution.py:107
  62.0 9.2 broadcast_select_fusion
  71.2 190.7 %all_to_all.42 = bf16[32,64,2048]{2,1,0:T(8,128)(2,1)} all-to-all(bf16[32,64,2048]{2,1,0:T(8,128)(2,1)S(1)} %get-tuple-element.16), channel_id=1, replica_groups=mesh['expert'=8,'replica'=4] {'expert','replica'}, dimensions={0} | all-to-all | bytes 16777216 | tf_op jit(solution)/shard_map/all_to_all | solution.py:81
  272.8 11.8 %fusion.31 = f32[2048,768]{1,0:T(8,128)} fusion(bf16[2048,2048]{1,0:T(8,128)(2,1)} %bitcast.101, bf16[2048,1152]{0,1:T(8,128)(2,1)} %bitcast.94), kind=kOutput, calls=%fused_computation.59 | convolution fusion | flops 6442450944 | bytes 17825792 | tf_op jit(solution)/shard_map/dot_general | solution.py:21
  284.6 167.6 %all-to-all-done.2 = bf16[32,64,2048]{2,1,0:T(8,128)(2,1)} async-done(((bf16[32,64,2048]{2,1,0:T(8,128)(2,1)}), bf16[32,64,2048]{2,1,0:T(8,128)(2,1)}, u32[]{:S(2)}, u32[]{:S(2)}) %all-to-all-start.2) | async-done | bytes 8388640 | tf_op jit(solution)/shard_map/all_to_all | solution.py:81
  452.2 12.8 %multiply_convert_fusion.1 = (bf16[2048,384]{1,0:T(8,128)(2,1)S(1)}, bf16[2048,384]{1,0:T(8,128)(2,1)S(1)}, bf16[2048,384]{1,0:T(8,128)(2,1)}) fusion(f32[2048,768]{1,0:T(8,128)} %fusion.31, bf16[2048,2048]{1,0:T(8,128)(2,1)} %bitcast.14, bf16[2048,1152]{0,1:T(8,128)(2,1)} %bitcast.95), kind=kOutput, calls=%fused_computation.55 | convolution fusion | flops 3233808384 | bytes 20971520 | tf_op jit(solution)/shard_map/dot_general | solution.py:38
  465.0 9.0 convolution_convert_fusion
  474.0 14.4 %all-to-all-start.3 = ((bf16[32,64,2048]{2,1,0:T(8,128)(2,1)}), bf16[32,64,2048]{2,1,0:T(8,128)(2,1)}, u32[]{:S(2)}, u32[]{:S(2)}) async-start(bf16[32,64,2048]{2,1,0:T(8,128)(2,1)} %bitcast.103), calls=%async_computation.3 | async-start | bytes 16777216 | tf_op jit(solution)/shard_map/all_to_all | solution.py:85
  488.4 9.8 %convolution_convert_fusion.1 = bf16[2048,2048]{1,0:T(8,128)(2,1)} fusion(bf16[2048,384]{1,0:T(8,128)(2,1)} %get-tuple-element.12, bf16[2048,1152]{0,1:T(8,128)(2,1)} %bitcast.96), kind=kOutput, calls=%fused_computation.41 | convolution fusion | flops 3225419776 | bytes 11534336 | tf_op jit(solution)/shard_map/dot_general | solution.py:25
  498.1 176.3 %all-to-all-done.3 = bf16[32,64,2048]{2,1,0:T(8,128)(2,1)} async-done(((bf16[32,64,2048]{2,1,0:T(8,128)(2,1)}), bf16[32,64,2048]{2,1,0:T(8,128)(2,1)}, u32[]{:S(2)}, u32[]{:S(2)}) %all-to-all-start.3) | async-done | bytes 8388640 | tf_op jit(solution)/shard_map/all_to_all | solution.py:85
  678.2 6.7 copy.35
  692.4 9.9 %bitcast_convert_fusion.1 = bf16[4,2048,384]{1,2,0:T(8,128)(2,1)} fusion(bf16[8,4,64,2048]{3,2,1,0:T(8,128)(2,1)} %bitcast.24, bf16[8,4,64,384]{3,2,1,0:T(8,128)(2,1)} %bitcast.116), kind=kOutput, calls=%fused_computation.11 | convolution fusion | flops 3224371200 | bytes 16252928 | tf_op jit(solution)/shard_map/arcd,arcf->rdf/dot_general | solution.py:60
  702.3 12.4 %bitcast_convert_fusion = bf16[4,2048,768]{1,2,0:T(8,128)(2,1)} fusion(bf16[8,4,64,2048]{3,2,1,0:T(8,128)(2,1)} %bitcast.102, bf16[8,4,64,384]{3,2,1,0:T(8,128)(2,1)} %bitcast.115, bf16[8,4,64,384]{3,2,1,0:T(8,128)(2,1)S(1)} %bitcast.114), kind=kOutput, calls=%fused_computation.7 | convolution fusion | flops 6455033856 | bytes 24117248 | tf_op jit(solution)/shard_map/arcd,arcg->rdg/dot_general | solution.py:54
  714.7 20.3 %pad_maximum_fusion = bf16[4,2048,1152]{1,2,0:T(8,128)(2,1)} fusion(bf16[4,2048,384]{1,2,0:T(8,128)(2,1)} %bitcast_convert_fusion.1, bf16[4,2048,768]{1,2,0:T(8,128)(2,1)} %bitcast_convert_fusion), kind=kLoop, calls=%fused_computation.8 | loop fusion | flops 37748736 | bytes 37748736 | tf_op jit(solution)/shard_map/concatenate | solution.py:67
  735.0 14.7 %convert_reduce_fusion = f32[2048,1152]{0,1:T(8,128)} fusion(bf16[4,2048,1152]{1,2,0:T(8,128)(2,1)} %pad_maximum_fusion), kind=kLoop, calls=%fused_computation.6 | loop fusion | flops 16515072 | bytes 28311552 | tf_op jit(solution)/shard_map/reduce_sum | solution.py:69
  749.7 6.8 multiply_reduce_fusion
  757.2 14.3 %select_bitcast_fusion = bf16[1,2048,1152]{1,2,0:T(8,128)(2,1)} fusion(pred[]{:T(512)S(6)} %eq.36, bf16[1,2048,1152]{1,2,0:T(8,128)(2,1)} %copy.36, f32[2048,1152]{0,1:T(8,128)} %convert_reduce_fusion, f32[]{:T(128)S(6)} %min.3, bf16[1,2048,1152]{1,2,0:T(8,128)(2,1)} %copy.35, bf16[1,2048,1152]{1,2,0:T(8,128)(2,1)} %copy.32), kind=kLoop, calls=%fused_computation.42 | loop fusion | flops 44826624 | bytes 28311556 | tf_op jit(solution)/shard_map/broadcast_in_dim | solution.py:135
  771.5 14.5 %fusion.18 = bf16[1,2048,1152]{1,2,0:T(8,128)(2,1)} fusion(bf16[1,2048,1152]{1,2,0:T(8,128)(2,1)} %copy.36, bf16[1,2048,1152]{1,2,0:T(8,128)(2,1)} %copy.35, bf16[1,2048,1152]{1,2,0:T(8,128)(2,1)} %copy.32, f32[2048,1152]{0,1:T(8,128)} %convert_reduce_fusion, f32[]{:T(128)S(6)} %min.3), kind=kLoop, calls=%fused_computation.35 | loop fusion | flops 42467328 | bytes 28311556 | tf_op jit(solution)/shard_map/convert_element_type | solution.py:133
  786.1 6.6 copy.37
  792.7 102.5 %all-reduce.2.cloned.1.call-done = bf16[1,2048,1152]{1,2,0:T(8,128)(2,1)} async-done(((bf16[1,2048,1152]{1,2,0:T(8,128)(2,1)}), bf16[1,2048,1152]{1,2,0:T(8,128)(2,1)}) %all-reduce.2.cloned.1.call-update) | async-done | bytes 4718608 | tf_op jit(solution)/shard_map/psum | solution.py:17
  901.9 13.5 %gather_fusion.3 = bf16[1024,2048]{1,0:T(8,128)(2,1)} fusion(bf16[2048,2048]{1,0:T(8,128)(2,1)} %bitcast.16, s32[1024]{0:T(1024)S(1)} %broadcast_clamp_fusion), kind=kCustom, calls=%fused_computation.3 | custom fusion | bytes 8392704 | tf_op jit(solution)/shard_map/gather | solution.py:121
  921.3 13.3 %gather_fusion.1 = bf16[1024,2048]{1,0:T(8,128)(2,1)} fusion(bf16[2048,2048]{1,0:T(8,128)(2,1)} %bitcast.8, s32[1024]{0:T(1024)S(1)} %broadcast_clamp_fusion), kind=kCustom, calls=%fused_computation.1 | custom fusion | bytes 8392704 | tf_op jit(solution)/shard_map/gather | solution.py:109
  (54 shorter events, 57.6 us)
Async XLA Ops:
  7.2 43.8 %copy-start = (bf16[128,2048]{1,0:T(8,128)(2,1)S(1)}, bf16[128,2048]{1,0:T(8,128)(2,1)}, u32[]{:S(2)}) copy-start(bf16[128,2048]{1,0:T(8,128)(2,1)} %param.8) | copy-start | bytes 1572868
  261.9 190.3 %all-to-all-start.2 = ((bf16[32,64,2048]{2,1,0:T(8,128)(2,1)}), bf16[32,64,2048]{2,1,0:T(8,128)(2,1)}, u32[]{:S(2)}, u32[]{:S(2)}) async-start(bf16[32,64,2048]{2,1,0:T(8,128)(2,1)} %get-tuple-element.15), calls=%async_computation.2 | async-start | bytes 16777216 | tf_op jit(solution)/shard_map/all_to_all | solution.py:81
  452.2 12.8 %copy-start.2 = (bf16[1,2048,1152]{1,2,0:T(8,128)(2,1)S(1)}, bf16[1,2048,1152]{1,2,0:T(8,128)(2,1)}, u32[]{:S(2)}) copy-start(bf16[1,2048,1152]{1,2,0:T(8,128)(2,1)} %copy.32) | copy-start | bytes 14155780
  465.0 9.0 copy-start.6
  474.0 200.5 %all-to-all-start.3 = ((bf16[32,64,2048]{2,1,0:T(8,128)(2,1)}), bf16[32,64,2048]{2,1,0:T(8,128)(2,1)}, u32[]{:S(2)}, u32[]{:S(2)}) async-start(bf16[32,64,2048]{2,1,0:T(8,128)(2,1)} %bitcast.103), calls=%async_computation.3 | async-start | bytes 16777216 | tf_op jit(solution)/shard_map/all_to_all | solution.py:85
  674.5 246.8 %all-to-all-start.1 = ((bf16[32,64,2048]{2,1,0:T(8,128)(2,1)}), bf16[32,64,2048]{2,1,0:T(8,128)(2,1)}, u32[]{:S(2)}, u32[]{:S(2)}) async-start(bf16[32,64,2048]{2,1,0:T(8,128)(2,1)} %bitcast.100), calls=%async_computation.1 | async-start | bytes 16777216 | tf_op jit(solution)/shard_map/all_to_all | solution.py:85
  678.2 217.1 %all-reduce.2.cloned.1.call-start = ((), (), s32[]{:S(2)}) async-start(), calls=%async_computation.4 | async-start | bytes 9437184 | tf_op jit(solution)/shard_map/psum | solution.py:17
  685.0 7.3 copy-start.5
  934.6 4.7 copy-start.3
  934.6 4.7 copy-start.4
  934.6 8.0 copy-start.1
Sparse Core Ops, SparseCore 0:
  771.7 123.5 all-reduce.1
where the time goes:
time: 958 us; the launch traced here: 950 us
  waiting for transfers between devices  446 us (47%)
  blocking collectives  191 us (20%)
  local copies, waits for them, and re-layouts  103 us (11%)
  other arithmetic  99.2 us (10%)
  matrix products  71.9 us (8%)
  starting transfers between devices  22.4 us (2%)
  between operations  16 us (2%)
    all_to_all x1, blocking collectives, to_experts(): lax.all_to_all(row_block, ('expert', 'replica'), split_axis=0, concat_axi...  191 us
    all_to_all x2, waiting for transfers between devices, from_experts(): lax.all_to_all(row_block, ('expert', 'replica'), split_axis=0, concat_axi...  176 us
    all_to_all x1, waiting for transfers between devices, to_experts(): lax.all_to_all(row_block, ('expert', 'replica'), split_axis=0, concat_axi...  168 us
    psum x1, waiting for transfers between devices, broadcast(): return lax.psum(kept, axis)  103 us
    unnamed x22, local copies, waits for them, and re-layouts  35 us
    concatenate x1, other arithmetic, partial_sums(): jnp.concatenate([in_part, down_part], axis=2).astype(jnp.bfloat16)  20.3 us
  transfers between devices with their start and end apart: 4, of which 3 were waited for; matrix products, arithmetic and copies ran while one was open for 18% of the time, Pallas kernels for 0%

commit v1 on v0

v1 whole, which is shorter than its diff:
```python
import jax
import jax.numpy as jnp
from jax import lax
from jax.sharding import PartitionSpec as P

beta_first = 0.9
beta_second = 0.95
adam_eps = 1e-08
rate = 0.05
clip_norm = 1.0
bias_first = 1.0 - 0.9**10
bias_second = 1.0 - 0.95**10
BOTH = ("expert", "replica")
F32 = jnp.float32
BF16 = jnp.bfloat16


class Grid:
    def __init__(self, groups, owners):
        self.line = groups // 2
        self.sides = owners // 2
        self.owners = owners
        self.count = groups * owners

    def split(self, device):
        place, owner = device // self.owners, device % self.owners
        return place // 2, place % 2, owner // 2, owner % 2

    def join(self, line, row, side, core):
        return ((line * 2 + row) * self.sides + side) * 2 + core

    def move(self, value, step):
        pairs = [(d, self.join(*step(*self.split(d)))) for d in range(self.count)]
        return lax.ppermute(value, BOTH, pairs)

    def up(self, value):
        return self.move(value, lambda z, y, x, c: ((z + 1) % self.line, y, x, c))

    def down(self, value):
        return self.move(value, lambda z, y, x, c: ((z - 1) % self.line, y, x, c))

    def cross_a(self, value):
        return self.move(value, lambda z, y, x, c: (z, y ^ (1 - c), x ^ c, c))

    def cross_b(self, value):
        return self.move(value, lambda z, y, x, c: (z, y ^ c, x ^ (1 - c), c))

    def cross_side(self, value):
        return self.move(value, lambda z, y, x, c: (z, y, x ^ 1, c))

    def cross_core(self, value):
        return self.move(value, lambda z, y, x, c: (z, y, x, c ^ 1))


def chunk_compute(slots, select, row_gate, weights, width):
    blocks, room, token_count = select.shape[1:]
    stacked = jnp.stack(slots)
    rows = jnp.einsum(
        "eqjt,qtd->eqjd", select, stacked[:, :token_count], preferred_element_type=BF16
    )
    cots = jnp.einsum(
        "eqjt,qtd->eqjd", select, stacked[:, token_count:], preferred_element_type=BF16
    )
    kept, mixed, dx, grads = [], [], [], []
    for e in range(2):
        row_e = rows[e].reshape(blocks * room, -1)
        cot_e = cots[e].reshape(blocks * room, -1)
        gate = row_gate[e].reshape(blocks * room, 1)
        gate_up = jnp.dot(row_e, weights[e][:, : 2 * width], preferred_element_type=F32)
        spread = jnp.dot(cot_e, weights[e][:, 2 * width :], preferred_element_type=F32)
        gate_in, up_in = gate_up[:, :width], gate_up[:, width:]
        sig = jax.nn.sigmoid(gate_in)
        hidden = gate_in * sig * up_in
        grads.append(jnp.sum(hidden * spread, axis=1).reshape(blocks, room))
        hidden_gated = (hidden * gate).astype(BF16)
        hidden_grad = spread * gate
        both = jnp.concatenate(
            [hidden_grad * up_in * sig * (1.0 + gate_in * (1.0 - sig)), hidden_grad * gate_in * sig],
            axis=1,
        ).astype(BF16)
        nt = (((1,), (1,)), ((), ()))
        mixed.append(
            lax.dot_general(
                hidden_gated, weights[e][:, 2 * width :], nt, preferred_element_type=F32
            ).astype(BF16)
        )
        dx.append(
            lax.dot_general(
                both, weights[e][:, : 2 * width], nt, preferred_element_type=F32
            ).astype(BF16)
        )
        kept.append((row_e, cot_e, both, hidden_gated))
    mixed = jnp.stack(mixed).reshape(2, blocks, room, -1)
    dx = jnp.stack(dx).reshape(2, blocks, room, -1)
    mixed_part = jnp.einsum("eqjt,eqjd->qtd", select, mixed, preferred_element_type=F32)
    dx_part = jnp.einsum("eqjt,eqjd->qtd", select, dx, preferred_element_type=F32)
    parts = jnp.concatenate([mixed_part, dx_part], axis=1).astype(BF16)
    return [parts[q] for q in range(blocks)], kept, jnp.stack(grads)


def add(*values):
    total = values[0].astype(F32)
    for value in values[1:]:
        total = total + value.astype(F32)
    return total


def shards(
    tokens, expert_ids, gates, cotangent, expert_weights, moment_first, moment_second, hot_slot
):
    groups = lax.axis_size("expert")
    owners = lax.axis_size("replica")
    experts = groups * owners
    grid = Grid(groups, owners)
    line = grid.line
    token_count, chosen = expert_ids.shape
    width = expert_weights.shape[2] // 3
    room = 2 * token_count * chosen // experts
    device = lax.axis_index("expert") * owners + lax.axis_index("replica")
    z, y, x, c = grid.split(device)
    weights = expert_weights[0]

    expert_range = jnp.arange(experts, dtype=jnp.int32)
    hit = expert_ids[:, :, None] == expert_range
    gate_table = jnp.sum(jnp.where(hit, gates[:, :, None], 0.0), axis=1).T
    by_chip = gate_table.reshape(experts // 2, 1, 2, token_count)
    send = jnp.broadcast_to(by_chip, (experts // 2, 2, 2, token_count))
    table = lax.all_to_all(
        send.reshape(experts, 2 * token_count), BOTH, split_axis=0, concat_axis=0, tiled=True
    ).reshape(experts, 2, token_count)
    steps = jnp.arange(line, dtype=jnp.int32)[:, None]
    flip_a = jnp.array([0, 1, 0, 1], jnp.int32)[None]
    flip_b = jnp.array([0, 0, 1, 1], jnp.int32)[None]
    flip_y = jnp.where(c == 0, flip_a, flip_b)
    flip_x = jnp.where(c == 0, flip_b, flip_a)
    source = grid.join((z - steps) % line, y ^ flip_y, x ^ flip_x, c)
    gate_slot = table[source]
    gate_slot = jnp.where(c == 0, gate_slot, gate_slot[:, :, ::-1])
    taken = gate_slot > 0.0
    before = jnp.triu(jnp.ones((token_count, token_count), BF16), 1)
    ahead = jnp.dot(taken.astype(BF16), before, preferred_element_type=F32).astype(jnp.int32)
    slot = jnp.where(taken, ahead, room)
    picked = slot[:, :, :, None, :] == jnp.arange(room, dtype=jnp.int32)[:, None]
    select = picked.astype(BF16).transpose(0, 2, 1, 3, 4)
    row_gate = jnp.sum(jnp.where(picked, gate_slot[:, :, :, None, :], 0.0), axis=4).transpose(
        0, 2, 1, 3
    )

    other = grid.cross_core(weights)
    pair = (weights, other)
    current = jnp.concatenate([tokens, cotangent], axis=0)
    parts, kept, dots = [], [], []
    for r in range(line):
        near_a = grid.cross_a(current)
        near_b = grid.cross_b(current)
        far = grid.cross_b(near_a)
        part, keep, dot = chunk_compute(
            [current, near_a, near_b, far], select[r], row_gate[r], pair, width
        )
        parts.append(part)
        kept.append(keep)
        dots.append(dot)
        if r + 1 < line:
            current = grid.up(current)

    carried = None
    for r in reversed(range(line)):
        own, near_a, near_b, far = parts[r]
        passed = grid.cross_b(far)
        from_b = grid.cross_b(near_b)
        from_a = grid.cross_a(add(near_a, passed).astype(BF16))
        terms = [own, from_b, from_a] + ([carried] if carried is not None else [])
        total = add(*terms)
        if r:
            carried = grid.down(total.astype(BF16))
    result = total.astype(BF16)
    mixed, input_grad = result[:token_count], result[token_count:]

    dot_slot = jnp.stack(dots)
    dot_token = jnp.sum(
        select.astype(F32) * dot_slot[..., None], axis=3
    )
    dz, dy, dx_, _ = grid.split(expert_range)
    turn_y, turn_x = dy ^ y, dx_ ^ x
    kind_a = jnp.where(c == 0, turn_y, turn_x)
    kind_b = jnp.where(c == 0, turn_x, turn_y)
    back = dot_token.transpose(0, 2, 1, 3).reshape(line * 4, 2, token_count)[
        ((z - dz) % line) * 4 + kind_a + 2 * kind_b
    ]
    returned = lax.all_to_all(
        back.reshape(experts, 2 * token_count), BOTH, split_axis=0, concat_axis=0, tiled=True
    ).reshape(experts // 2, 2, 2, token_count)
    lane = jnp.where(c == 0, returned[:, 0], returned[:, 1, ::-1]).reshape(experts, token_count)
    gate_grad = jnp.sum(jnp.where(hit, lane.T[:, None, :], 0.0), axis=2)

    grad = []
    for e in range(2):
        row_e, cot_e, both, hidden = (
            jnp.concatenate([kept[r][e][i] for r in range(line)]) for i in range(4)
        )
        tn = (((0,), (0,)), ((), ()))
        grad.append(
            jnp.concatenate(
                [
                    lax.dot_general(row_e, both, tn, preferred_element_type=F32),
                    lax.dot_general(cot_e, hidden, tn, preferred_element_type=F32),
                ],
                axis=1,
            )
        )
    gradient = grad[0] + grid.cross_core(grad[1].astype(BF16)).astype(F32)
    clip_bound = clip_norm * experts ** (-0.5)
    scale = jnp.minimum(1.0, clip_bound / (jnp.sqrt(jnp.sum(gradient * gradient)) + 1e-06))
    scaled = scale * gradient
    first = beta_first * moment_first[0].astype(F32) + (1.0 - beta_first) * scaled
    second = beta_second * moment_second[0].astype(F32) + (1.0 - beta_second) * scaled * scaled
    update = first / bias_first / (jnp.sqrt(second / bias_second) + adam_eps)
    new_weights = (weights.astype(F32) - rate * update).astype(BF16)

    hot = hot_slot[0]
    new_other = grid.cross_core(new_weights)
    candidate = jnp.where(hot % 2 == c, new_weights, new_other)
    half = candidate.shape[0] // 2
    piece = grid.cross_side(lax.dynamic_slice_in_dim(candidate, c * half, half, 0))
    piece_other = grid.cross_core(piece)
    across = jnp.where(
        c == 0,
        jnp.concatenate([piece, piece_other]),
        jnp.concatenate([piece_other, piece]),
    )
    hot_copy = jnp.where(hot // 2 == x, candidate, across)
    return (mixed, input_grad, gate_grad, new_weights[None], hot_copy[None])


def solution(mesh):
    return jax.shard_map(
        shards,
        mesh=mesh,
        in_specs=(
            P(BOTH, None),
            P(BOTH, None),
            P(BOTH, None),
            P(BOTH, None),
            P(BOTH, None, None),
            P(BOTH, None, None),
            P(BOTH, None, None),
            P("expert"),
        ),
        out_specs=(
            P(BOTH, None),
            P(BOTH, None),
            P(BOTH, None),
            P(BOTH, None, None),
            P(BOTH, None, None),
        ),
        check_vma=False,
    )
```

time: 958 us -> 465 us (0.49)
  waiting for transfers between devices: 446 us -> 191 us
  blocking collectives: 191 us -> 0 us
  local copies, waits for them, and re-layouts: 103 us -> 50.6 us
  other arithmetic: 99.2 us -> 63.9 us
  starting transfers between devices: 22.4 us -> 53.1 us
  matrix products: 71.9 us -> 96 us
  between operations: 16 us -> 3.62 us
    all_to_all x3 -> x2, waiting for transfers between devices: 344 us -> 21.4 us  [the longest x1 21.4 us: shards(): lax.all_to_all(back.reshape(experts, 2 * token_count), BOTH, split_axis=0...]
    all_to_all x1 -> x0, blocking collectives: 191 us -> none  [to_experts(): lax.all_to_all(row_block, ('expert', 'replica'), split_axis=0, concat_axi...]
    ppermute x0 -> x35, waiting for transfers between devices: none -> 170 us  [move(): return lax.ppermute(value, BOTH, pairs)]
    psum x1 -> x0, waiting for transfers between devices: 103 us -> none  [broadcast(): return lax.psum(kept, axis)]
    gather x4, local copies, waits for them, and re-layouts: 56.9 us -> 1.82 us  [the longest x1 1.22 us: shards(): dot_token.transpose(0, 2, 1, 3).reshape(line * 4, 2, token_count)]
    ppermute x0 -> x35, starting transfers between devices: none -> 47.5 us  [move(): return lax.ppermute(value, BOTH, pairs)]
    dot_general x8 -> x53, matrix products: 71.9 us -> 96 us  [the longest x8 20.6 us: chunk_compute(): lax.dot_general(both, weights[e][:, :2 * width], nt, preferred_element_ty...]
    concatenate x1, other arithmetic: 20.3 us -> 0.71 us  [shards(): jnp.concatenate([lax.dot_general(row_e, both, tn, preferred_element_type=...]
  transfers between devices with their start and end apart: 4 -> 37, of which waited for: 3 -> 13; matrix products, arithmetic and copies ran while one was open for 18% -> 37% of each run, Pallas kernels for 0% -> 0%
where the time goes in v1:
time: 465 us; the launch traced here: 458 us
  waiting for transfers between devices  191 us (41%)
  matrix products  96 us (21%)
  other arithmetic  63.9 us (14%)
  starting transfers between devices  53.1 us (11%)
  local copies, waits for them, and re-layouts  50.6 us (11%)
    ppermute x35, waiting for transfers between devices, move(): return lax.ppermute(value, BOTH, pairs)  170 us
    ppermute x35, starting transfers between devices, move(): return lax.ppermute(value, BOTH, pairs)  47.5 us
    unnamed x154, local copies, waits for them, and re-layouts  39 us
    all_to_all x1, waiting for transfers between devices, shards(): lax.all_to_all(back.reshape(experts, 2 * token_count), BOTH, split_axis=0...  21.4 us
    dot_general x8, matrix products, chunk_compute(): lax.dot_general(both, weights[e][:, :2 * width], nt, preferred_element_ty...  20.6 us
    dot_general x8, matrix products, chunk_compute(): lax.dot_general(hidden_gated, weights[e][:, 2 * width:], nt, preferred_el...  16.3 us
    dot_general x8, matrix products, chunk_compute(): jnp.dot(cot_e, weights[e][:, 2 * width:], preferred_element_type=F32)  15.7 us
    dot_general x8, matrix products, chunk_compute(): jnp.dot(row_e, weights[e][:, :2 * width], preferred_element_type=F32)  15.7 us
  transfers between devices with their start and end apart: 37, of which 13 were waited for; matrix products, arithmetic and copies ran while one was open for 37% of the time, Pallas kernels for 0%

profile of v1, /device:TPU:0, one launch (start us, length us, event | category | flops | bytes accessed | tf_op | source)
XLA Modules:
  0.0 458.4 jit_solution(3074751661349134010)
XLA Ops:
  13.2 6.6 %copy.139 = bf16[1,2048,1152]{1,2,0:T(8,128)(2,1)} copy(bf16[1,2048,1152]{2,1,0:T(8,128)(2,1)} %param.14) | data formatting | bytes 9437184 | tf_op args[4]
  20.1 8.0 %collective-permute-done = bf16[256,2048]{1,0:T(8,128)(2,1)} collective-permute-done((bf16[256,2048]{1,0:T(8,128)(2,1)S(1)}, bf16[256,2048]{1,0:T(8,128)(2,1)}, u32[]{:S(2)}, u32[]{:S(2)}) %collective-permute-start) | collective-permute-done | bytes 1048608 | tf_op jit(solution)/shard_map/ppermute | solution.py:34
  32.5 6.6 %copy.162 = bf16[1,2048,1152]{1,2,0:T(8,128)(2,1)} copy(bf16[1,2048,1152]{2,1,0:T(8,128)(2,1)} %param.16) | data formatting | bytes 9437184 | tf_op args[6]
  39.1 6.6 %copy.161 = bf16[1,2048,1152]{1,2,0:T(8,128)(2,1)} copy(bf16[1,2048,1152]{2,1,0:T(8,128)(2,1)} %param.15) | data formatting | bytes 9437184 | tf_op args[5]
  55.0 20.7 %collective-permute-done.8 = bf16[256,2048]{1,0:T(8,128)(2,1)S(1)} collective-permute-done((bf16[256,2048]{1,0:T(8,128)(2,1)S(1)}, bf16[256,2048]{1,0:T(8,128)(2,1)S(1)}, u32[]{:S(2)}, u32[]{:S(2)}) %collective-permute-start.8) | collective-permute-done | bytes 1048608 | tf_op jit(solution)/shard_map/ppermute | solution.py:34
  86.7 15.1 %collective-permute-done.10 = bf16[256,2048]{1,0:T(8,128)(2,1)S(1)} collective-permute-done((bf16[256,2048]{1,0:T(8,128)(2,1)S(1)}, bf16[256,2048]{1,0:T(8,128)(2,1)S(1)}, u32[]{:S(2)}, u32[]{:S(2)}) %collective-permute-start.10) | collective-permute-done | bytes 1048608 | tf_op jit(solution)/shard_map/ppermute | solution.py:34
  105.2 4.4 collective-permute-done.15
  116.5 15.6 %collective-permute-done.22 = bf16[256,2048]{1,0:T(8,128)(2,1)S(1)} collective-permute-done((bf16[256,2048]{1,0:T(8,128)(2,1)S(1)}, bf16[256,2048]{1,0:T(8,128)(2,1)S(1)}, u32[]{:S(2)}, u32[]{:S(2)}) %collective-permute-start.22) | collective-permute-done | bytes 1048608 | tf_op jit(solution)/shard_map/ppermute | solution.py:34
  152.7 4.0 convolution_convert_fusion.10
  174.4 5.2 %fusion.43 = bf16[2048,768]{0,1:T(8,128)(2,1)S(1)} fusion(bf16[256,2048]{1,0:T(8,128)(2,1)} %bitcast.381, bf16[256,2048]{1,0:T(8,128)(2,1)S(1)} %bitcast.370, bf16[256,2048]{1,0:T(8,128)(2,1)S(1)} %bitcast.363, bf16[256,2048]{1,0:T(8,128)(2,1)S(1)} %bitcast.352, bf16[256,384]{1,0:T(8,128)(2,1)} %get-tuple-element.77, ...), kind=kOutput, calls=%fused_computation.88 | convolution fusion | flops 3252158464 | bytes 8912896 | tf_op jit(solution)/shard_map/dot_general | solution.py:205
  192.8 3.9 convolution_convert_fusion.12
  213.8 6.5 %multiply_reduce_fusion = f32[]{:T(128)} fusion(bf16[2048,1152]{0,1:T(8,128)(2,1)} %collective-permute-done.31, f32[2048,384]{0,1:T(8,128)} %fusion.19, f32[2048,768]{0,1:T(8,128)S(1)} %fusion.11), kind=kLoop, calls=%fused_computation.13 | loop fusion | flops 11796479 | bytes 14155780 | tf_op jit(solution)/shard_map/reduce_sum | solution.py:213
  221.0 13.8 %fusion.8 = bf16[2048,1152]{0,1:T(8,128)(2,1)S(1)} fusion(bf16[1,2048,1152]{1,2,0:T(8,128)(2,1)} %copy.162, bf16[1,2048,1152]{1,2,0:T(8,128)(2,1)} %copy.161, bf16[2048,1152]{0,1:T(8,128)(2,1)} %collective-permute-done.31, f32[2048,384]{0,1:T(8,128)} %fusion.19, f32[2048,768]{0,1:T(8,128)} %copy-done.12, f32[]{:T(128)S(6)} %min.3, ...), kind=kLoop, calls=%fused_computation.14 | loop fusion | flops 49545216 | bytes 33030148 | tf_op jit(solution)/shard_map/convert_element_type | solution.py:218
  252.1 4.3 collective-permute-done.26
  264.4 12.4 %collective-permute-done.25 = bf16[256,2048]{1,0:T(8,128)(2,1)S(1)} collective-permute-done((bf16[256,2048]{1,0:T(8,128)(2,1)S(1)}, bf16[256,2048]{1,0:T(8,128)(2,1)S(1)}, u32[]{:S(2)}, u32[]{:S(2)}) %collective-permute-start.25) | collective-permute-done | bytes 1048608 | tf_op jit(solution)/shard_map/ppermute | solution.py:34
  277.3 5.7 %collective-permute-done.27 = bf16[256,2048]{1,0:T(8,128)(2,1)S(1)} collective-permute-done((bf16[256,2048]{1,0:T(8,128)(2,1)S(1)}, bf16[256,2048]{1,0:T(8,128)(2,1)S(1)}, u32[]{:S(2)}, u32[]{:S(2)}) %collective-permute-start.27) | collective-permute-done | bytes 1048608 | tf_op jit(solution)/shard_map/ppermute | solution.py:34
  283.5 3.8 collective-permute-start.28
  287.2 5.1 %broadcast_select_fusion = bf16[2048,1152]{0,1:T(8,128)(2,1)} fusion(bf16[2048,1152]{0,1:T(8,128)(2,1)S(1)} %fusion.8, bf16[2048,1152]{0,1:T(8,128)(2,1)} %collective-permute-done.32, pred[]{:T(512)S(6)} %eq.74), kind=kLoop, calls=%fused_computation.43 | loop fusion | flops 2359296 | bytes 14155777 | tf_op jit(solution)/shard_map/jit(_where)/select_n | solution.py:222
  311.1 4.3 collective-permute-start.29
  315.9 79.2 %collective-permute-done.5 = bf16[256,2048]{1,0:T(8,128)(2,1)} collective-permute-done((bf16[256,2048]{1,0:T(8,128)(2,1)}, bf16[256,2048]{1,0:T(8,128)(2,1)}, u32[]{:S(2)}, u32[]{:S(2)}) %collective-permute-start.5) | collective-permute-done | bytes 1048608 | tf_op jit(solution)/shard_map/ppermute | solution.py:34
  410.3 21.4 %all-to-all-done.1 = f32[32,1,256]{2,1,0:T(1,128)S(1)} async-done(((f32[32,1,256]{2,1,0:T(1,128)}), f32[32,1,256]{2,1,0:T(1,128)S(1)}, u32[]{:S(2)}, u32[]{:S(2)}) %all-to-all-start.1) | async-done | bytes 32800 | tf_op jit(solution)/shard_map/all_to_all | solution.py:190
  432.4 6.6 %copy.163 = bf16[1,2048,1152]{2,1,0:T(8,128)(2,1)} copy(bf16[1,2048,1152]{1,2,0:T(8,128)(2,1)} %bitcast.319) | data formatting | bytes 9437184
  442.8 8.8 %fusion.10 = bf16[1,2048,1152]{1,2,0:T(8,128)(2,1)} fusion(bf16[2048,1152]{0,1:T(8,128)(2,1)} %broadcast_select_fusion, bf16[1024,1152]{0,1:T(8,128)(2,1)} %collective-permute-done.34, bf16[1024,1152]{0,1:T(8,128)(2,1)} %collective-permute-done.33, pred[]{:T(512)S(6)} %eq.62, pred[]{:T(512)S(6)} %eq.73), kind=kLoop, calls=%fused_computation.42 | loop fusion | flops 23592960 | bytes 14155778 | tf_op jit(solution)/shard_map/broadcast_in_dim | solution.py:232
  451.6 6.6 %copy.164 = bf16[1,2048,1152]{2,1,0:T(8,128)(2,1)} copy(bf16[1,2048,1152]{1,2,0:T(8,128)(2,1)} %fusion.10) | data formatting | bytes 9437184
  (336 shorter events, 179.5 us)
Async XLA Ops:
  5.8 42.2 %collective-permute-start.7 = (bf16[256,2048]{1,0:T(8,128)(2,1)S(1)}, bf16[256,2048]{1,0:T(8,128)(2,1)S(1)}, u32[]{:S(2)}, u32[]{:S(2)}) collective-permute-start(bf16[256,2048]{1,0:T(8,128)(2,1)S(1)} %constant_dynamic-update-slice_fusion), channel_id=1, source_target_pairs={{0,8},{1,9},{2,10},{3,11},{4,12},{5,13},{6,14},{7,15},{8,16},{9,17... | collective-permute-start | bytes 3145736 | tf_op jit(solution)/shard_map/ppermute | solution.py:34
  7.4 43.8 %collective-permute-start.1 = (bf16[256,2048]{1,0:T(8,128)(2,1)S(1)}, bf16[256,2048]{1,0:T(8,128)(2,1)}, u32[]{:S(2)}, u32[]{:S(2)}) collective-permute-start(bf16[256,2048]{1,0:T(8,128)(2,1)S(1)} %constant_dynamic-update-slice_fusion), channel_id=1, source_target_pairs={{0,2},{1,5},{2,0},{3,7},{4,6},{5,1},{6,4},{7,3},{8,10},{9,13},{10,... | collective-permute-start | bytes 3145736 | tf_op jit(solution)/shard_map/ppermute | solution.py:34
  10.2 35.5 %all-to-all-start = ((f32[32,1,256]{2,1,0:T(1,128)}), f32[32,1,256]{2,1,0:T(1,128)S(1)}, u32[]{:S(2)}, u32[]{:S(2)}) async-start(f32[32,1,256]{2,1,0:T(1,128)} %bitcast.2), calls=%async_computation | async-start | bytes 65536 | tf_op jit(solution)/shard_map/all_to_all | solution.py:128
  19.9 121.2 %collective-permute-start.3 = (bf16[2048,1152]{0,1:T(8,128)(2,1)}, bf16[2048,1152]{0,1:T(8,128)(2,1)}, u32[]{:S(2)}, u32[]{:S(2)}) collective-permute-start(bf16[2048,1152]{0,1:T(8,128)(2,1)} %bitcast.320), channel_id=1, source_target_pairs={{0,1},{1,0},{2,3},{3,2},{4,5},{5,4},{6,7},{7,6},{8,9},{9,8},{10,11... | collective-permute-start | bytes 14155784 | tf_op jit(solution)/shard_map/ppermute | solution.py:34
  48.0 28.9 %collective-permute-start.14 = (bf16[256,2048]{1,0:T(8,128)(2,1)S(1)}, bf16[256,2048]{1,0:T(8,128)(2,1)S(1)}, u32[]{:S(2)}, u32[]{:S(2)}) collective-permute-start(bf16[256,2048]{1,0:T(8,128)(2,1)S(1)} %collective-permute-done.7), channel_id=1, source_target_pairs={{0,8},{1,9},{2,10},{3,11},{4,12},{5,13},{6,14},{7,15},{8,16},{9,17... | collective-permute-start | bytes 3145736 | tf_op jit(solution)/shard_map/ppermute | solution.py:34
  51.2 33.4 %collective-permute-start.9 = (bf16[256,2048]{1,0:T(8,128)(2,1)S(1)}, bf16[256,2048]{1,0:T(8,128)(2,1)S(1)}, u32[]{:S(2)}, u32[]{:S(2)}) collective-permute-start(bf16[256,2048]{1,0:T(8,128)(2,1)S(1)} %collective-permute-done.7), channel_id=1, source_target_pairs={{0,2},{1,5},{2,0},{3,7},{4,6},{5,1},{6,4},{7,3},{8,10},{9,13},{10,... | collective-permute-start | bytes 3145736 | tf_op jit(solution)/shard_map/ppermute | solution.py:34
  84.7 47.4 %collective-permute-start.16 = (bf16[256,2048]{1,0:T(8,128)(2,1)S(1)}, bf16[256,2048]{1,0:T(8,128)(2,1)S(1)}, u32[]{:S(2)}, u32[]{:S(2)}) collective-permute-start(bf16[256,2048]{1,0:T(8,128)(2,1)S(1)} %collective-permute-done.14), channel_id=1, source_target_pairs={{0,2},{1,5},{2,0},{3,7},{4,6},{5,1},{6,4},{7,3},{8,10},{9,13},{10,... | collective-permute-start | bytes 3145736 | tf_op jit(solution)/shard_map/ppermute | solution.py:34
  103.8 28.3 %collective-permute-start.22 = (bf16[256,2048]{1,0:T(8,128)(2,1)S(1)}, bf16[256,2048]{1,0:T(8,128)(2,1)S(1)}, u32[]{:S(2)}, u32[]{:S(2)}) collective-permute-start(bf16[256,2048]{1,0:T(8,128)(2,1)S(1)} %collective-permute-done.21), channel_id=1, source_target_pairs={{0,4},{1,3},{2,6},{3,1},{4,0},{5,7},{6,2},{7,5},{8,12},{9,11},{10,... | collective-permute-start | bytes 3145736 | tf_op jit(solution)/shard_map/ppermute | solution.py:34
  110.7 52.0 %collective-permute-start.23 = (bf16[256,2048]{1,0:T(8,128)(2,1)S(1)}, bf16[256,2048]{1,0:T(8,128)(2,1)S(1)}, u32[]{:S(2)}, u32[]{:S(2)}) collective-permute-start(bf16[256,2048]{1,0:T(8,128)(2,1)S(1)} %collective-permute-done.21), channel_id=1, source_target_pairs={{0,2},{1,5},{2,0},{3,7},{4,6},{5,1},{6,4},{7,3},{8,10},{9,13},{10,... | collective-permute-start | bytes 3145736 | tf_op jit(solution)/shard_map/ppermute | solution.py:34
  132.1 30.6 %collective-permute-start.24 = (bf16[256,2048]{1,0:T(8,128)(2,1)S(1)}, bf16[256,2048]{1,0:T(8,128)(2,1)S(1)}, u32[]{:S(2)}, u32[]{:S(2)}) collective-permute-start(bf16[256,2048]{1,0:T(8,128)(2,1)S(1)} %collective-permute-done.22), channel_id=1, source_target_pairs={{0,2},{1,5},{2,0},{3,7},{4,6},{5,1},{6,4},{7,3},{8,10},{9,13},{10,... | collective-permute-start | bytes 3145736 | tf_op jit(solution)/shard_map/ppermute | solution.py:34
  180.3 30.9 %collective-permute-start.31 = (bf16[2048,1152]{0,1:T(8,128)(2,1)S(1)}, bf16[2048,1152]{0,1:T(8,128)(2,1)}, u32[]{:S(2)}, u32[]{:S(2)}) collective-permute-start(bf16[2048,1152]{0,1:T(8,128)(2,1)S(1)} %pad_maximum_fusion), channel_id=1, source_target_pairs={{0,1},{1,0},{2,3},{3,2},{4,5},{5,4},{6,7},{7,6},{8,9},{9,8},{10,11... | collective-permute-start | bytes 14155784 | tf_op jit(solution)/shard_map/ppermute | solution.py:34
  186.2 73.4 %collective-permute-start.19 = (bf16[256,2048]{1,0:T(8,128)(2,1)}, bf16[256,2048]{1,0:T(8,128)(2,1)}, u32[]{:S(2)}, u32[]{:S(2)}) collective-permute-start(bf16[256,2048]{1,0:T(8,128)(2,1)} %get-tuple-element.43), channel_id=1, source_target_pairs={{0,2},{1,5},{2,0},{3,7},{4,6},{5,1},{6,4},{7,3},{8,10},{9,13},{10,... | collective-permute-start | bytes 3145736 | tf_op jit(solution)/shard_map/ppermute | solution.py:34
  188.0 115.9 %collective-permute-start.18 = (bf16[256,2048]{1,0:T(8,128)(2,1)}, bf16[256,2048]{1,0:T(8,128)(2,1)}, u32[]{:S(2)}, u32[]{:S(2)}) collective-permute-start(bf16[256,2048]{1,0:T(8,128)(2,1)} %get-tuple-element.42), channel_id=1, source_target_pairs={{0,2},{1,5},{2,0},{3,7},{4,6},{5,1},{6,4},{7,3},{8,10},{9,13},{10,... | collective-permute-start | bytes 3145736 | tf_op jit(solution)/shard_map/ppermute | solution.py:34
  234.9 52.3 %collective-permute-start.32 = (bf16[2048,1152]{0,1:T(8,128)(2,1)S(1)}, bf16[2048,1152]{0,1:T(8,128)(2,1)}, u32[]{:S(2)}, u32[]{:S(2)}) collective-permute-start(bf16[2048,1152]{0,1:T(8,128)(2,1)S(1)} %fusion.8), channel_id=1, source_target_pairs={{0,1},{1,0},{2,3},{3,2},{4,5},{5,4},{6,7},{7,6},{8,9},{9,8},{10,11... | collective-permute-start | bytes 14155784 | tf_op jit(solution)/shard_map/ppermute | solution.py:34
  259.7 39.8 %collective-permute-start.12 = (bf16[256,2048]{1,0:T(8,128)(2,1)}, bf16[256,2048]{1,0:T(8,128)(2,1)}, u32[]{:S(2)}, u32[]{:S(2)}) collective-permute-start(bf16[256,2048]{1,0:T(8,128)(2,1)} %get-tuple-element.41), channel_id=1, source_target_pairs={{0,2},{1,5},{2,0},{3,7},{4,6},{5,1},{6,4},{7,3},{8,10},{9,13},{10,... | collective-permute-start | bytes 3145736 | tf_op jit(solution)/shard_map/ppermute | solution.py:34
  295.6 103.7 %collective-permute-start.33 = (bf16[1024,1152]{0,1:T(8,128)(2,1)}, bf16[1024,1152]{0,1:T(8,128)(2,1)}, u32[]{:S(2)}, u32[]{:S(2)}) collective-permute-start(bf16[1024,1152]{0,1:T(8,128)(2,1)} %constant_dynamic-slice_fusion), channel_id=1, source_target_pairs={{0,2},{1,3},{2,0},{3,1},{4,6},{5,7},{6,4},{7,5},{8,10},{9,11},{10,... | collective-permute-start | bytes 7077896 | tf_op jit(solution)/shard_map/ppermute | solution.py:34
  299.5 99.2 %collective-permute-start.11 = (bf16[256,2048]{1,0:T(8,128)(2,1)}, bf16[256,2048]{1,0:T(8,128)(2,1)}, u32[]{:S(2)}, u32[]{:S(2)}) collective-permute-start(bf16[256,2048]{1,0:T(8,128)(2,1)} %get-tuple-element.40), channel_id=1, source_target_pairs={{0,2},{1,5},{2,0},{3,7},{4,6},{5,1},{6,4},{7,3},{8,10},{9,13},{10,... | collective-permute-start | bytes 3145736 | tf_op jit(solution)/shard_map/ppermute | solution.py:34
  303.8 91.2 %collective-permute-start.5 = (bf16[256,2048]{1,0:T(8,128)(2,1)}, bf16[256,2048]{1,0:T(8,128)(2,1)}, u32[]{:S(2)}, u32[]{:S(2)}) collective-permute-start(bf16[256,2048]{1,0:T(8,128)(2,1)} %get-tuple-element.39), channel_id=1, source_target_pairs={{0,2},{1,5},{2,0},{3,7},{4,6},{5,1},{6,4},{7,3},{8,10},{9,13},{10,... | collective-permute-start | bytes 3145736 | tf_op jit(solution)/shard_map/ppermute | solution.py:34
  304.3 95.0 %collective-permute-start.13 = (bf16[256,2048]{1,0:T(8,128)(2,1)}, bf16[256,2048]{1,0:T(8,128)(2,1)}, u32[]{:S(2)}, u32[]{:S(2)}) collective-permute-start(bf16[256,2048]{1,0:T(8,128)(2,1)} %fusion.80), channel_id=1, source_target_pairs={{0,4},{1,3},{2,6},{3,1},{4,0},{5,7},{6,2},{7,5},{8,12},{9,11},{10,... | collective-permute-start | bytes 3145736 | tf_op jit(solution)/shard_map/ppermute | solution.py:34
  311.1 88.2 %collective-permute-start.29 = (bf16[256,2048]{1,0:T(8,128)(2,1)}, bf16[256,2048]{1,0:T(8,128)(2,1)}, u32[]{:S(2)}, u32[]{:S(2)}) collective-permute-start(bf16[256,2048]{1,0:T(8,128)(2,1)} %fusion.79), channel_id=1, source_target_pairs={{0,24},{1,25},{2,26},{3,27},{4,28},{5,29},{6,30},{7,31},{8,0},{9,1... | collective-permute-start | bytes 3145736 | tf_op jit(solution)/shard_map/ppermute | solution.py:34
  395.1 44.0 %collective-permute-start.4 = (bf16[256,2048]{1,0:T(8,128)(2,1)}, bf16[256,2048]{1,0:T(8,128)(2,1)}, u32[]{:S(2)}, u32[]{:S(2)}) collective-permute-start(bf16[256,2048]{1,0:T(8,128)(2,1)} %get-tuple-element.38), channel_id=1, source_target_pairs={{0,2},{1,5},{2,0},{3,7},{4,6},{5,1},{6,4},{7,3},{8,10},{9,13},{10,... | collective-permute-start | bytes 3145736 | tf_op jit(solution)/shard_map/ppermute | solution.py:34
  398.6 40.4 %collective-permute-start.6 = (bf16[256,2048]{1,0:T(8,128)(2,1)S(1)}, bf16[256,2048]{1,0:T(8,128)(2,1)}, u32[]{:S(2)}, u32[]{:S(2)}) collective-permute-start(bf16[256,2048]{1,0:T(8,128)(2,1)S(1)} %fusion.84), channel_id=1, source_target_pairs={{0,4},{1,3},{2,6},{3,1},{4,0},{5,7},{6,2},{7,5},{8,12},{9,11},{10,... | collective-permute-start | bytes 3145736 | tf_op jit(solution)/shard_map/ppermute | solution.py:34
  399.3 43.5 %collective-permute-start.34 = (bf16[1024,1152]{0,1:T(8,128)(2,1)}, bf16[1024,1152]{0,1:T(8,128)(2,1)}, u32[]{:S(2)}, u32[]{:S(2)}) collective-permute-start(bf16[1024,1152]{0,1:T(8,128)(2,1)} %collective-permute-done.33), channel_id=1, source_target_pairs={{0,1},{1,0},{2,3},{3,2},{4,5},{5,4},{6,7},{7,6},{8,9},{9,8},{10,11... | collective-permute-start | bytes 7077896 | tf_op jit(solution)/shard_map/ppermute | solution.py:34
  402.9 36.1 %collective-permute-start.30 = (bf16[256,2048]{1,0:T(8,128)(2,1)}, bf16[256,2048]{1,0:T(8,128)(2,1)}, u32[]{:S(2)}, u32[]{:S(2)}) collective-permute-start(bf16[256,2048]{1,0:T(8,128)(2,1)} %fusion.83), channel_id=1, source_target_pairs={{0,24},{1,25},{2,26},{3,27},{4,28},{5,29},{6,30},{7,31},{8,0},{9,1... | collective-permute-start | bytes 3145736 | tf_op jit(solution)/shard_map/ppermute | solution.py:34
  (87 other events, 860.0 us)
